TPU v7x, 256 devices: a whole 4x4x8 slice. The times are simulated.
256 devices in a mesh: hid: 32 (over y, z), wid: 4 (over x), ad: 2 (over core).
Axes of the slice: x: 4, y: 4, z: 8, core: 2. Of those that a mesh axis runs over, the one named last changes fastest.
Arguments:
- activations: bfloat16 [1536, 2, 8192], P(None, None, ('wid', 'ad')), may hold values from -6 to 6
- row_adapter_index: int32 [1536, 2], replicated, may hold values from 0 to 127, as said below
- gate_up_weight: bfloat16 [8192, 2, 14848], P(('wid', 'ad'), None, 'hid'), may hold values from -0.0625 to 0.0625
- down_weight: bfloat16 [14848, 8192], P('hid', ('wid', 'ad')), may hold values from -0.046875 to 0.046875
- adapter_shrink_weight: bfloat16 [128, 2, 64, 8192], P(('hid', 'wid'), 'ad'), may hold values from -0.0625 to 0.0625
- adapter_expand_weight: bfloat16 [128, 2, 64, 14848], P(('hid', 'wid'), 'ad'), may hold values from -0.75 to 0.75
Outputs:
- layer_out: bfloat16 [1536, 2, 8192], P('hid', None, ('wid', 'ad'))
Inputs may be any that keep to these rules, and one draw needn't show every extreme that they name: `row_adapter_index`: call rows 48 * h to 48 * h + 47 of both batches together block h. In every block no adapter is named more than 2 times, and one and the same adapter is named exactly 2 times in every block.
All inputs are finite; a program needn't handle non-finite values.
Results may differ from a plain program's by a relative error of at most 0.0064.
Values may be sent and summed in bfloat16 or wider, within the bound.
No kernel may reach another device: no remote copies, remote signals or barrier semaphores. Data moves between devices by JAX's collectives and lax.ppermute only.
A program may use at most 128 MiB of HBM per device.

v0:
```python
import jax
import jax.numpy as jnp
from jax import lax
from jax.sharding import Mesh, PartitionSpec as P

CHUNKS = 3
Y, Z = (4, 8)
F32 = jnp.float32
BF16 = jnp.bfloat16


def local(activations, row_adapter_index, gate_up_weight, down_weight, shrink, expand):
    hid = lax.axis_index(("y", "z"))
    wid = lax.axis_index("wid")
    ad = lax.axis_index("ad")
    n_hid = Y * Z
    total_rows, batches, width = activations.shape
    rows = total_rows * batches
    block = rows // n_hid
    part = block // CHUNKS
    units = down_weight.shape[0]
    rank = shrink.shape[2]
    slots = 2 * n_hid
    by_owner = expand[0, 0].reshape(rank, n_hid, units).transpose(1, 0, 2)
    expand_all = lax.all_to_all(by_owner, ("y", "z"), split_axis=0, concat_axis=0, tiled=True)

    def to_chunks(flat):
        return flat.reshape((n_hid, CHUNKS, part) + flat.shape[1:]).swapaxes(0, 1)

    acts = activations.reshape(n_hid, CHUNKS, part // 2, 2, width)
    acts = acts.swapaxes(0, 1).reshape(rows, width)
    ids = row_adapter_index.reshape(n_hid, block)
    same = ids[:, :, None] == ids[:, None, :]
    earlier = jnp.arange(block)[None, :] < jnp.arange(block)[:, None]
    place = jnp.sum((same & earlier[None]).astype(jnp.int32), axis=2)
    slot = 2 * jnp.arange(n_hid, dtype=jnp.int32)[:, None] + place
    owner, cls = (ids // 4, ids % 4)
    send_code = jnp.where(owner == hid, cls * slots + slot, -1)
    recv_code = jnp.where(cls == wid, owner * slots + slot, -1)
    send_code = to_chunks(send_code.reshape(rows)).reshape(rows)
    recv_code = to_chunks(recv_code.reshape(rows)).reshape(CHUNKS, rows // CHUNKS)
    pick = (jnp.arange(4 * slots, dtype=jnp.int32)[:, None] == send_code[None, :]).astype(BF16)
    picked = jnp.dot(pick, acts, preferred_element_type=F32).astype(BF16)
    picked = picked.reshape(4, 1, slots, width)
    picked = jnp.broadcast_to(picked, (4, 2, slots, width)).reshape(8, slots, width)
    got = lax.all_to_all(picked, ("wid", "ad"), split_axis=0, concat_axis=0, tiled=True)
    inner = jnp.einsum(
        "xsf,jxf->sj", got, shrink[0, 0].reshape(rank, 8, width), preferred_element_type=F32
    ).astype(BF16)
    inner_all = lax.all_to_all(
        jnp.broadcast_to(inner[None], (n_hid, slots, rank)),
        ("y", "z"),
        split_axis=0,
        concat_axis=0,
        tiled=True,
    )
    terms = (
        jnp.einsum("hsj,hju->hsu", inner_all, expand_all, preferred_element_type=F32)
        .astype(BF16)
        .reshape(n_hid * slots, units)
    )
    weights = gate_up_weight.transpose(1, 0, 2)
    chunk_rows = rows // CHUNKS
    half = chunk_rows // 2
    quarter = half // 4
    is_mine = (jnp.arange(2) == ad)[:, None, None]
    swap = [(0, 1), (1, 0)]
    acts = acts.reshape(CHUNKS, chunk_rows, width)
    outs = []
    for c in range(CHUNKS):
        base = jnp.einsum("rd,pdu->pru", acts[c], weights, preferred_element_type=F32)
        place_rows = (
            recv_code[c][:, None] == jnp.arange(n_hid * slots, dtype=jnp.int32)[None, :]
        ).astype(BF16)
        delta = jnp.dot(place_rows, terms, preferred_element_type=F32).astype(BF16)
        value = base + jnp.where(is_mine, delta.astype(F32)[None], 0.0)
        away = lax.dynamic_slice_in_dim(value, (1 - ad) * half, half, 1).astype(BF16)
        keep = lax.dynamic_slice_in_dim(value, ad * half, half, 1)
        pair = keep + lax.ppermute(away, "ad", swap).astype(F32)
        pair = pair.astype(BF16).reshape(2, 4, quarter, units).swapaxes(0, 1)
        parts = lax.all_to_all(pair, "wid", split_axis=0, concat_axis=0, tiled=True)
        summed = jnp.sum(parts.astype(F32), axis=0)
        hidden = (jax.nn.silu(summed[0]) * summed[1]).astype(BF16)
        hidden = lax.all_gather(hidden, ("ad", "wid"), axis=0, tiled=True)
        partial = jnp.dot(hidden, down_weight, preferred_element_type=F32).astype(BF16)
        partial = lax.psum_scatter(partial, "y", scatter_dimension=0, tiled=True)
        outs.append(lax.psum_scatter(partial, "z", scatter_dimension=0, tiled=True))
    out = jnp.concatenate(outs, axis=0)
    return out.reshape(total_rows // n_hid, batches, -1)


def solution(mesh):
    grid = Mesh(mesh.devices.reshape(Y, Z, 4, 2), ("y", "z", "wid", "ad"))
    hid = ("y", "z")
    in_specs = (
        P(None, None, ("wid", "ad")),
        P(),
        P(("wid", "ad"), None, hid),
        P(hid, ("wid", "ad")),
        P(("y", "z", "wid"), "ad", None, None),
        P(("y", "z", "wid"), "ad", None, None),
    )
    return jax.shard_map(
        local, mesh=grid, in_specs=in_specs, out_specs=P(hid, None, ("wid", "ad")), check_vma=False
    )
```

profile of v0, /device:TPU:2, one launch (start us, length us, event | category | flops | bytes accessed | tf_op | source)
XLA Modules:
  0.0 464.6 jit_solution(17052631867190961436)
XLA Ops:
  10.0 6.8 %copy.57 = bf16[32,3,16,2,1024]{4,3,2,0,1:T(2,128)(2,1)} copy(bf16[32,3,16,2,1024]{4,3,2,1,0:T(2,128)(2,1)} %bitcast.107) | data formatting | bytes 12582912 | tf_op jit(solution)/shard_map/reshape | solution.py:30
  16.7 10.2 %reshape.89 = bf16[3072,1024]{1,0:T(8,128)(2,1)} reshape(bf16[3,32,16,2,1024]{4,3,2,1,0:T(2,128)(2,1)} %bitcast.104) | data formatting | bytes 12582912 | tf_op jit(solution)/shard_map/reshape | solution.py:31
  26.9 4.6 fusion.17
  32.7 6.4 %all-to-all-start = ((bf16[8,64,1024]{2,1,0:T(8,128)(2,1)}), bf16[8,64,1024]{2,1,0:T(8,128)(2,1)}, u32[]{:S(2)}, u32[]{:S(2)}) async-start(bf16[8,64,1024]{2,1,0:T(8,128)(2,1)} %bitcast.7), calls=%async_computation | async-start | bytes 2097152 | tf_op jit(solution)/shard_map/all_to_all | solution.py:46
  40.7 13.0 %all-to-all-done = bf16[8,64,1024]{2,1,0:T(8,128)(2,1)} async-done(((bf16[8,64,1024]{2,1,0:T(8,128)(2,1)}), bf16[8,64,1024]{2,1,0:T(8,128)(2,1)}, u32[]{:S(2)}, u32[]{:S(2)}) %all-to-all-start) | async-done | bytes 1048608 | tf_op jit(solution)/shard_map/all_to_all | solution.py:46
  53.6 2.9 fusion.18
  57.8 9.9 %all-to-all-start.1 = ((bf16[32,2,2048]{2,1,0:T(2,128)(2,1)}), bf16[32,2,2048]{2,1,0:T(2,128)(2,1)S(1)}, u32[]{:S(2)}, u32[]{:S(2)}) async-start(bf16[32,2,2048]{2,1,0:T(2,128)(2,1)} %reshape.120), calls=%async_computation.1 | async-start | bytes 524288 | tf_op jit(solution)/shard_map/all_to_all | solution.py:50
  67.7 6.7 %reshape_squeeze.7 = bf16[64,32,464]{2,1,0:T(8,128)(2,1)} reshape(bf16[1,1,64,14848]{3,2,1,0:T(8,128)(2,1)} %param.11) | data formatting | bytes 3801088 | tf_op jit(solution)/shard_map/reshape;squeeze | solution.py:24
  74.4 4.1 copy.58
  79.8 8.8 %all-to-all-start.2 = ((bf16[32,64,464]{2,1,0:T(8,128)(2,1)}), bf16[32,64,464]{2,1,0:T(8,128)(2,1)}, u32[]{:S(2)}, u32[]{:S(2)}) async-start(bf16[32,64,464]{2,1,0:T(8,128)(2,1)} %bitcast.106), calls=%async_computation.2 | async-start | bytes 4194304 | tf_op jit(solution)/shard_map/all_to_all | solution.py:25
  88.8 7.7 %fusion.30 = (bf16[1,32,16,2,1024]{4,3,2,1,0:T(2,128)(2,1)}, bf16[1,32,16,2,1024]{4,3,2,1,0:T(2,128)(2,1)}, bf16[1,32,16,2,1024]{4,3,2,1,0:T(2,128)(2,1)}) fusion(bf16[3,32,16,2,1024]{4,3,2,1,0:T(2,128)(2,1)} %bitcast.105), kind=kLoop, calls=%fused_computation.79 | loop fusion | bytes 12582912 | tf_op jit(solution)/shard_map/slice | solution.py:71
  96.5 4.1 reshape.96
  100.9 36.9 %all-to-all-done.2 = bf16[32,64,464]{2,1,0:T(8,128)(2,1)} async-done(((bf16[32,64,464]{2,1,0:T(8,128)(2,1)}), bf16[32,64,464]{2,1,0:T(8,128)(2,1)}, u32[]{:S(2)}, u32[]{:S(2)}) %all-to-all-start.2) | async-done | bytes 1900576 | tf_op jit(solution)/shard_map/all_to_all | solution.py:25
  148.2 2.6 collective-permute-done
  150.8 3.0 bitcast_bitcast_fusion.2
  153.8 4.9 %all-to-all-start.3 = ((bf16[4,2,128,464]{2,3,1,0:T(8,128)(2,1)}), bf16[4,2,128,464]{2,3,1,0:T(8,128)(2,1)S(1)}, u32[]{:S(2)}, u32[]{:S(2)}) async-start(bf16[4,2,128,464]{2,3,1,0:T(8,128)(2,1)} %bitcast_bitcast_fusion.2), calls=%async_computation.3 | async-start | bytes 1900544 | tf_op jit(solution)/shard_map/all_to_all | solution.py:81
  158.8 4.1 reshape.99
  162.9 9.0 %all-to-all-done.3 = bf16[4,2,128,464]{2,3,1,0:T(8,128)(2,1)S(1)} async-done(((bf16[4,2,128,464]{2,3,1,0:T(8,128)(2,1)}), bf16[4,2,128,464]{2,3,1,0:T(8,128)(2,1)S(1)}, u32[]{:S(2)}, u32[]{:S(2)}) %all-to-all-start.3) | async-done | bytes 950304 | tf_op jit(solution)/shard_map/all_to_all | solution.py:81
  172.1 24.2 %all_gather.9 = bf16[1024,464]{0,1:T(8,128)(2,1)S(1)} all-gather(bf16[128,464]{0,1:T(8,128)(2,1)S(1)} %fusion.28), channel_id=1, replica_groups=mesh['y'=4,'z'=8,'wid'=4,'ad'=2] {'ad','wid'}, dimensions={0}, use_global_device_ids=true | all-gather | bytes 1069056 | tf_op jit(solution)/shard_map/all_gather | solution.py:84
  196.4 2.6 convolution_convert_fusion.2
  199.0 4.1 fusion.12
  209.7 4.9 %all-to-all-start.5 = ((bf16[4,2,128,464]{2,3,1,0:T(8,128)(2,1)}), bf16[4,2,128,464]{2,3,1,0:T(8,128)(2,1)S(1)}, u32[]{:S(2)}, u32[]{:S(2)}) async-start(bf16[4,2,128,464]{2,3,1,0:T(8,128)(2,1)} %bitcast_bitcast_fusion), calls=%async_computation.9 | async-start | bytes 1900544 | tf_op jit(solution)/shard_map/all_to_all | solution.py:81
  214.7 4.1 reshape.98
  218.8 9.2 %all-to-all-done.5 = bf16[4,2,128,464]{2,3,1,0:T(8,128)(2,1)S(1)} async-done(((bf16[4,2,128,464]{2,3,1,0:T(8,128)(2,1)}), bf16[4,2,128,464]{2,3,1,0:T(8,128)(2,1)S(1)}, u32[]{:S(2)}, u32[]{:S(2)}) %all-to-all-start.5) | async-done | bytes 950304 | tf_op jit(solution)/shard_map/all_to_all | solution.py:81
  228.2 24.1 %all_gather.11 = bf16[1024,464]{0,1:T(8,128)(2,1)S(1)} all-gather(bf16[128,464]{0,1:T(8,128)(2,1)S(1)} %fusion.24), channel_id=1, replica_groups=mesh['y'=4,'z'=8,'wid'=4,'ad'=2] {'ad','wid'}, dimensions={0}, use_global_device_ids=true | all-gather | bytes 1069056 | tf_op jit(solution)/shard_map/all_gather | solution.py:84
  255.3 4.1 fusion.14
  265.3 17.4 %all_to_all.30 = bf16[4,2,128,464]{2,3,1,0:T(8,128)(2,1)S(1)} all-to-all(bf16[4,2,128,464]{2,3,1,0:T(8,128)(2,1)S(1)} %bitcast_bitcast_fusion.1), channel_id=1, replica_groups=mesh['y'=4,'z'=8,'wid'=4,'ad'=2] {'wid'}, dimensions={0} | all-to-all | bytes 1900544 | tf_op jit(solution)/shard_map/all_to_all | solution.py:81
  282.9 23.9 %all_gather.10 = bf16[1024,464]{0,1:T(8,128)(2,1)S(1)} all-gather(bf16[128,464]{0,1:T(8,128)(2,1)S(1)} %fusion.26), channel_id=1, replica_groups=mesh['y'=4,'z'=8,'wid'=4,'ad'=2] {'ad','wid'}, dimensions={0}, use_global_device_ids=true | all-gather | bytes 1069056 | tf_op jit(solution)/shard_map/all_gather | solution.py:84
  310.6 28.0 %reduce-scatter.11.cloned.1.call-done = bf16[256,1024]{1,0:T(8,128)(2,1)} async-done(((bf16[1024,1024]{1,0:T(8,128)(2,1)}), bf16[256,1024]{1,0:T(8,128)(2,1)}) %reduce-scatter.11.cloned.1.call-update) | async-done | bytes 524304 | tf_op jit(solution)/shard_map/reduce_scatter | solution.py:86
  338.7 39.8 %reduce-scatter.9.cloned.1.call-done = bf16[32,1024]{1,0:T(8,128)(2,1)} async-done(((bf16[256,1024]{1,0:T(8,128)(2,1)}), bf16[32,1024]{1,0:T(8,128)(2,1)}) %reduce-scatter.9.cloned.1.call-update) | async-done | bytes 65552 | tf_op jit(solution)/shard_map/reduce_scatter | solution.py:87
  378.5 38.8 %reduce-scatter.17.cloned.1.call-done = bf16[32,1024]{1,0:T(8,128)(2,1)} async-done(((bf16[256,1024]{1,0:T(8,128)(2,1)}), bf16[32,1024]{1,0:T(8,128)(2,1)}) %reduce-scatter.17.cloned.1.call-update) | async-done | bytes 65552 | tf_op jit(solution)/shard_map/reduce_scatter | solution.py:87
  417.3 38.8 %reduce-scatter.13.cloned.1.call-done = bf16[32,1024]{1,0:T(8,128)(2,1)} async-done(((bf16[256,1024]{1,0:T(8,128)(2,1)}), bf16[32,1024]{1,0:T(8,128)(2,1)}) %reduce-scatter.13.cloned.1.call-update) | async-done | bytes 65552 | tf_op jit(solution)/shard_map/reduce_scatter | solution.py:87
  (80 shorter events, 41.0 us)
Async XLA Ops:
  6.5 137.3 %copy-start = (bf16[1024,2,464]{0,2,1:T(8,128)(2,1)S(1)}, bf16[1024,2,464]{0,2,1:T(8,128)(2,1)}, u32[]{:S(2)}) copy-start(bf16[1024,2,464]{0,2,1:T(8,128)(2,1)} %param.8) | copy-start | bytes 5701636
  31.5 7.5 %copy-start.6 = (bf16[1,1,64,8192]{3,2,1,0:T(8,128)(2,1)S(1)}, bf16[1,1,64,8192]{3,2,1,0:T(8,128)(2,1)}, u32[]{:S(2)}) copy-start(bf16[1,1,64,8192]{3,2,1,0:T(8,128)(2,1)} %param.10) | copy-start | bytes 3145732
  32.7 21.0 %all-to-all-start = ((bf16[8,64,1024]{2,1,0:T(8,128)(2,1)}), bf16[8,64,1024]{2,1,0:T(8,128)(2,1)}, u32[]{:S(2)}, u32[]{:S(2)}) async-start(bf16[8,64,1024]{2,1,0:T(8,128)(2,1)} %bitcast.7), calls=%async_computation | async-start | bytes 2097152 | tf_op jit(solution)/shard_map/all_to_all | solution.py:46
  57.8 22.0 %all-to-all-start.1 = ((bf16[32,2,2048]{2,1,0:T(2,128)(2,1)}), bf16[32,2,2048]{2,1,0:T(2,128)(2,1)S(1)}, u32[]{:S(2)}, u32[]{:S(2)}) async-start(bf16[32,2,2048]{2,1,0:T(2,128)(2,1)} %reshape.120), calls=%async_computation.1 | async-start | bytes 524288 | tf_op jit(solution)/shard_map/all_to_all | solution.py:50
  79.8 58.0 %all-to-all-start.2 = ((bf16[32,64,464]{2,1,0:T(8,128)(2,1)}), bf16[32,64,464]{2,1,0:T(8,128)(2,1)}, u32[]{:S(2)}, u32[]{:S(2)}) async-start(bf16[32,64,464]{2,1,0:T(8,128)(2,1)} %bitcast.106), calls=%async_computation.2 | async-start | bytes 4194304 | tf_op jit(solution)/shard_map/all_to_all | solution.py:25
  140.1 1.3 copy-start.2
  141.4 2.4 copy-start.5
  146.1 1.8 copy-start.1
  148.0 2.7 collective-permute-start
  153.8 18.1 %all-to-all-start.3 = ((bf16[4,2,128,464]{2,3,1,0:T(8,128)(2,1)}), bf16[4,2,128,464]{2,3,1,0:T(8,128)(2,1)S(1)}, u32[]{:S(2)}, u32[]{:S(2)}) async-start(bf16[4,2,128,464]{2,3,1,0:T(8,128)(2,1)} %bitcast_bitcast_fusion.2), calls=%async_computation.3 | async-start | bytes 1900544 | tf_op jit(solution)/shard_map/all_to_all | solution.py:81
  158.7 150.8 %reduce-scatter.7.cloned.1.call-start = ((), (), s32[]{:S(2)}) async-start(), calls=%async_computation.12 | async-start | bytes 2621440 | tf_op jit(solution)/shard_map/reduce_scatter | solution.py:86
  171.9 24.5 %copy-start.7 = (bf16[464,1024]{1,0:T(8,128)(2,1)S(1)}, bf16[464,1024]{1,0:T(8,128)(2,1)}, u32[]{:S(2)}) copy-start(bf16[464,1024]{1,0:T(8,128)(2,1)} %param.9) | copy-start | bytes 2850820
  199.0 4.2 copy-start.4
  205.5 3.0 collective-permute-start.2
  209.7 18.3 %all-to-all-start.5 = ((bf16[4,2,128,464]{2,3,1,0:T(8,128)(2,1)}), bf16[4,2,128,464]{2,3,1,0:T(8,128)(2,1)S(1)}, u32[]{:S(2)}, u32[]{:S(2)}) async-start(bf16[4,2,128,464]{2,3,1,0:T(8,128)(2,1)} %bitcast_bitcast_fusion), calls=%async_computation.9 | async-start | bytes 1900544 | tf_op jit(solution)/shard_map/all_to_all | solution.py:81
  214.6 95.5 %reduce-scatter.15.cloned.1.call-start = ((), (), s32[]{:S(2)}) async-start(), calls=%async_computation.16 | async-start | bytes 2621440 | tf_op jit(solution)/shard_map/reduce_scatter | solution.py:86
  228.0 24.3 %copy-start.8 = (bf16[464,1024]{1,0:T(8,128)(2,1)S(1)}, bf16[464,1024]{1,0:T(8,128)(2,1)}, u32[]{:S(2)}) copy-start(bf16[464,1024]{1,0:T(8,128)(2,1)} %param.9) | copy-start | bytes 2850820
  254.9 83.7 %reduce-scatter.11.cloned.1.call-start = ((), (), s32[]{:S(2)}) async-start(), calls=%async_computation.14 | async-start | bytes 2621440 | tf_op jit(solution)/shard_map/reduce_scatter | solution.py:86
  255.2 4.2 copy-start.3
  261.7 3.3 collective-permute-start.1
  265.3 41.5 %copy-start.9 = (bf16[464,1024]{1,0:T(8,128)(2,1)S(1)}, bf16[464,1024]{1,0:T(8,128)(2,1)}, u32[]{:S(2)}) copy-start(bf16[464,1024]{1,0:T(8,128)(2,1)} %param.9) | copy-start | bytes 2850820
  309.4 69.1 %reduce-scatter.9.cloned.1.call-start = ((), (), s32[]{:S(2)}) async-start(), calls=%async_computation.13 | async-start | bytes 589824 | tf_op jit(solution)/shard_map/reduce_scatter | solution.py:87
  310.0 107.3 %reduce-scatter.17.cloned.1.call-start = ((), (), s32[]{:S(2)}) async-start(), calls=%async_computation.17 | async-start | bytes 589824 | tf_op jit(solution)/shard_map/reduce_scatter | solution.py:87
  310.6 145.5 %reduce-scatter.13.cloned.1.call-start = ((), (), s32[]{:S(2)}) async-start(), calls=%async_computation.15 | async-start | bytes 589824 | tf_op jit(solution)/shard_map/reduce_scatter | solution.py:87
Sparse Core Ops, SparseCore 0:
  199.1 29.3 reduce-scatter.6
  255.1 29.7 reduce-scatter.14
  309.5 29.0 reduce-scatter.10
  341.0 37.4 reduce-scatter.8
  380.9 36.3 reduce-scatter.16
  419.7 36.3 reduce-scatter.12
where the time goes:
time: 466 us; the launch traced here: 465 us
  waiting for transfers between devices  223 us (48%)
  blocking collectives  89.6 us (19%)
  local copies, waits for them, and re-layouts  58.9 us (13%)
  starting transfers between devices  37.5 us (8%)
  matrix products  34.8 us (7%)
  between operations  13.8 us (3%)
  other arithmetic  7.22 us (2%)
    reduce_scatter x3, waiting for transfers between devices, local(): outs.append(lax.psum_scatter(partial, 'z', scatter_dimension=0, tiled=True))  117 us
    all_gather x3, blocking collectives, local(): hidden = lax.all_gather(hidden, ('ad', 'wid'), axis=0, tiled=True)  72.3 us
    all_to_all x1, waiting for transfers between devices, local(): lax.all_to_all(by_owner, ('y', 'z'), split_axis=0, concat_axis=0, tiled=T...  36.9 us
    reduce_scatter x3, waiting for transfers between devices, local(): partial = lax.psum_scatter(partial, 'y', scatter_dimension=0, tiled=True)  28.1 us
    all_to_all x2, waiting for transfers between devices, local(): parts = lax.all_to_all(pair, 'wid', split_axis=0, concat_axis=0, tiled=True)  18.2 us
    all_to_all x1, blocking collectives, local(): parts = lax.all_to_all(pair, 'wid', split_axis=0, concat_axis=0, tiled=True)  17.4 us
    all_to_all x1, waiting for transfers between devices, local(): lax.all_to_all(picked, ('wid', 'ad'), split_axis=0, concat_axis=0, tiled=...  13 us
    squeeze x3, local copies, waits for them, and re-layouts, local(): acts[c]  12.4 us
  transfers between devices with their start and end apart: 14, of which 12 were waited for; matrix products, arithmetic and copies ran while one was open for 11% of the time, Pallas kernels for 0%

commit v1 on v0

--- a/solution.py
+++ b/solution.py
@@ -81,7 +81,15 @@
         parts = lax.all_to_all(pair, "wid", split_axis=0, concat_axis=0, tiled=True)
         summed = jnp.sum(parts.astype(F32), axis=0)
         hidden = (jax.nn.silu(summed[0]) * summed[1]).astype(BF16)
-        hidden = lax.all_gather(hidden, ("ad", "wid"), axis=0, tiled=True)
+        hidden = jnp.concatenate(
+            jax.lax.all_to_all(
+                jnp.stack(jax.lax.axis_size(("ad", "wid")) * [hidden], 0),
+                split_axis=0,
+                axis_name=("ad", "wid"),
+                concat_axis=0,
+            ),
+            0,
+        )
         partial = jnp.dot(hidden, down_weight, preferred_element_type=F32).astype(BF16)
         partial = lax.psum_scatter(partial, "y", scatter_dimension=0, tiled=True)
         outs.append(lax.psum_scatter(partial, "z", scatter_dimension=0, tiled=True))

time: 466 us -> 441 us (0.946)
  blocking collectives: 89.6 us -> 68.4 us
  waiting for transfers between devices: 223 us -> 211 us
  matrix products: 34.8 us -> 43.7 us
    all_gather x3 -> x0, blocking collectives: 72.3 us -> none  [local(): hidden = lax.all_gather(hidden, ('ad', 'wid'), axis=0, tiled=True)]
    all_to_all x1 -> x3, blocking collectives: 17.4 us -> 51.2 us  [local(): parts = lax.all_to_all(pair, 'wid', split_axis=0, concat_axis=0, tiled=True)]
    all_to_all x0 -> x1, blocking collectives: none -> 17.2 us  [local(): jax.lax.all_to_all(jnp.stack(jax.lax.axis_size(('ad', 'wid')) * [hidden],...]
    all_to_all x2, waiting for transfers between devices: 18.2 us -> 6.79 us  [local(): jax.lax.all_to_all(jnp.stack(jax.lax.axis_size(('ad', 'wid')) * [hidden],...]
  transfers between devices with their start and end apart: 14 -> 14, of which waited for: 12 -> 12; matrix products, arithmetic and copies ran while one was open for 11% -> 14% of each run, Pallas kernels for 0% -> 0%
where the time goes in v1:
time: 441 us; the launch traced here: 440 us
  waiting for transfers between devices  211 us (48%)
  blocking collectives  68.4 us (16%)
  local copies, waits for them, and re-layouts  61.1 us (14%)
  matrix products  43.7 us (10%)
  starting transfers between devices  36.3 us (8%)
  between operations  13.8 us (3%)
  other arithmetic  5.29 us (1%)
    reduce_scatter x3, waiting for transfers between devices, local(): outs.append(lax.psum_scatter(partial, 'z', scatter_dimension=0, tiled=True))  117 us
    all_to_all x3, blocking collectives, local(): parts = lax.all_to_all(pair, 'wid', split_axis=0, concat_axis=0, tiled=True)  51.2 us
    all_to_all x1, waiting for transfers between devices, local(): lax.all_to_all(by_owner, ('y', 'z'), split_axis=0, concat_axis=0, tiled=T...  36.9 us
    reduce_scatter x3, waiting for transfers between devices, local(): partial = lax.psum_scatter(partial, 'y', scatter_dimension=0, tiled=True)  27.9 us
    all_to_all x1, blocking collectives, local(): jax.lax.all_to_all(jnp.stack(jax.lax.axis_size(('ad', 'wid')) * [hidden],...  17.2 us
    dot_general x3, matrix products, local(): delta = jnp.dot(place_rows, terms, preferred_element_type=F32).astype(BF16)  13 us
    all_to_all x1, waiting for transfers between devices, local(): lax.all_to_all(picked, ('wid', 'ad'), split_axis=0, concat_axis=0, tiled=...  13 us
    squeeze x3, local copies, waits for them, and re-layouts, local(): acts[c]  12.4 us
  transfers between devices with their start and end apart: 14, of which 12 were waited for; matrix products, arithmetic and copies ran while one was open for 14% of the time, Pallas kernels for 0%

profile of v1, /device:TPU:2, one launch (start us, length us, event | category | flops | bytes accessed | tf_op | source)
XLA Modules:
  0.0 439.7 jit_solution(9856583019249585108)
XLA Ops:
  10.0 6.8 %copy.90 = bf16[32,3,16,2,1024]{4,3,2,0,1:T(2,128)(2,1)} copy(bf16[32,3,16,2,1024]{4,3,2,1,0:T(2,128)(2,1)} %bitcast.101) | data formatting | bytes 12582912 | tf_op jit(solution)/shard_map/reshape | solution.py:30
  16.8 10.2 %reshape.101 = bf16[3072,1024]{1,0:T(8,128)(2,1)} reshape(bf16[3,32,16,2,1024]{4,3,2,1,0:T(2,128)(2,1)} %bitcast.98) | data formatting | bytes 12582912 | tf_op jit(solution)/shard_map/reshape | solution.py:31
  27.0 4.6 %fusion.17 = bf16[256,1024]{1,0:T(8,128)(2,1)S(1)} fusion(bf16[3072,1024]{1,0:T(8,128)(2,1)} %reshape.101, s32[3072]{0:T(1024)S(1)} %eq.116), kind=kOutput, calls=%fused_computation.40 | convolution fusion | flops 1611661312 | bytes 6828032 | tf_op jit(solution)/shard_map/dot_general | solution.py:43
  32.7 6.4 %all-to-all-start = ((bf16[8,64,1024]{2,1,0:T(8,128)(2,1)}), bf16[8,64,1024]{2,1,0:T(8,128)(2,1)}, u32[]{:S(2)}, u32[]{:S(2)}) async-start(bf16[8,64,1024]{2,1,0:T(8,128)(2,1)} %bitcast.7), calls=%async_computation | async-start | bytes 2097152 | tf_op jit(solution)/shard_map/all_to_all | solution.py:46
  40.7 13.0 %all-to-all-done = bf16[8,64,1024]{2,1,0:T(8,128)(2,1)} async-done(((bf16[8,64,1024]{2,1,0:T(8,128)(2,1)}), bf16[8,64,1024]{2,1,0:T(8,128)(2,1)}, u32[]{:S(2)}, u32[]{:S(2)}) %all-to-all-start) | async-done | bytes 1048608 | tf_op jit(solution)/shard_map/all_to_all | solution.py:46
  57.8 9.9 %all-to-all-start.1 = ((bf16[32,2,2048]{2,1,0:T(2,128)(2,1)}), bf16[32,2,2048]{2,1,0:T(2,128)(2,1)S(1)}, u32[]{:S(2)}, u32[]{:S(2)}) async-start(bf16[32,2,2048]{2,1,0:T(2,128)(2,1)} %reshape.135), calls=%async_computation.1 | async-start | bytes 524288 | tf_op jit(solution)/shard_map/all_to_all | solution.py:50
  67.7 6.6 %reshape_squeeze.7 = bf16[64,32,464]{2,1,0:T(8,128)(2,1)} reshape(bf16[1,1,64,14848]{3,2,1,0:T(8,128)(2,1)} %param.11) | data formatting | bytes 3801088 | tf_op jit(solution)/shard_map/reshape;squeeze | solution.py:24
  74.4 4.1 copy.91
  79.8 8.7 %all-to-all-start.2 = ((bf16[32,64,464]{2,1,0:T(8,128)(2,1)}), bf16[32,64,464]{2,1,0:T(8,128)(2,1)}, u32[]{:S(2)}, u32[]{:S(2)}) async-start(bf16[32,64,464]{2,1,0:T(8,128)(2,1)} %bitcast.100), calls=%async_computation.2 | async-start | bytes 4194304 | tf_op jit(solution)/shard_map/all_to_all | solution.py:25
  88.7 7.7 %fusion.36 = (bf16[1,32,16,2,1024]{4,3,2,1,0:T(2,128)(2,1)}, bf16[1,32,16,2,1024]{4,3,2,1,0:T(2,128)(2,1)}, bf16[1,32,16,2,1024]{4,3,2,1,0:T(2,128)(2,1)}) fusion(bf16[3,32,16,2,1024]{4,3,2,1,0:T(2,128)(2,1)} %bitcast.99), kind=kLoop, calls=%fused_computation.82 | loop fusion | bytes 12582912 | tf_op jit(solution)/shard_map/slice | solution.py:71
  96.4 4.1 reshape.111
  100.9 36.9 %all-to-all-done.2 = bf16[32,64,464]{2,1,0:T(8,128)(2,1)} async-done(((bf16[32,64,464]{2,1,0:T(8,128)(2,1)}), bf16[32,64,464]{2,1,0:T(8,128)(2,1)}, u32[]{:S(2)}, u32[]{:S(2)}) %all-to-all-start.2) | async-done | bytes 1900576 | tf_op jit(solution)/shard_map/all_to_all | solution.py:25
  152.8 17.0 %all_to_all.45 = bf16[4,2,128,464]{2,3,1,0:T(8,128)(2,1)S(1)} all-to-all(bf16[4,2,128,464]{2,3,1,0:T(8,128)(2,1)S(1)} %bitcast_bitcast_fusion.2), channel_id=1, replica_groups=mesh['y'=4,'z'=8,'wid'=4,'ad'=2] {'wid'}, dimensions={0} | all-to-all | bytes 1900544 | tf_op jit(solution)/shard_map/all_to_all | solution.py:81
  171.0 4.9 %all-to-all-start.4 = ((bf16[8,128,464]{1,2,0:T(8,128)(2,1)}), bf16[8,128,464]{1,2,0:T(8,128)(2,1)S(1)}, u32[]{:S(2)}, u32[]{:S(2)}) async-start(bf16[8,128,464]{1,2,0:T(8,128)(2,1)} %stack.13), calls=%async_computation.4 | async-start | bytes 1900544 | tf_op jit(solution)/shard_map/all_to_all | solution.py:85
  176.0 4.1 reshape.114
  180.2 5.3 %fusion.12 = f32[1024,464]{0,1:T(8,128)} fusion(bf16[2048,464]{1,0:T(8,128)(2,1)} %bitcast.103, s32[1024]{0:T(1024)S(1)} %eq.123), kind=kOutput, calls=%fused_computation.35 | convolution fusion | flops 1949204480 | bytes 3805184 | tf_op jit(solution)/shard_map/dot_general | solution.py:75
  185.5 3.4 all-to-all-done.4
  188.9 3.8 convolution_convert_fusion.2
  192.7 4.3 bitcast_add_fusion
  200.0 17.1 %all_to_all.46 = bf16[4,2,128,464]{2,3,1,0:T(8,128)(2,1)S(1)} all-to-all(bf16[4,2,128,464]{2,3,1,0:T(8,128)(2,1)S(1)} %bitcast_bitcast_fusion), channel_id=1, replica_groups=mesh['y'=4,'z'=8,'wid'=4,'ad'=2] {'wid'}, dimensions={0} | all-to-all | bytes 1900544 | tf_op jit(solution)/shard_map/all_to_all | solution.py:81
  218.4 4.9 %all-to-all-start.8 = ((bf16[8,128,464]{1,2,0:T(8,128)(2,1)}), bf16[8,128,464]{1,2,0:T(8,128)(2,1)S(1)}, u32[]{:S(2)}, u32[]{:S(2)}) async-start(bf16[8,128,464]{1,2,0:T(8,128)(2,1)} %stack.17), calls=%async_computation.12 | async-start | bytes 1900544 | tf_op jit(solution)/shard_map/all_to_all | solution.py:85
  223.4 4.2 reshape.113
  227.5 5.3 %fusion.14 = f32[1024,464]{0,1:T(8,128)} fusion(bf16[2048,464]{1,0:T(8,128)(2,1)} %bitcast.104, s32[1024]{0:T(1024)S(1)} %eq.119), kind=kOutput, calls=%fused_computation.37 | convolution fusion | flops 1949204480 | bytes 3805184 | tf_op jit(solution)/shard_map/dot_general | solution.py:75
  232.8 3.4 all-to-all-done.8
  236.2 3.8 convolution_convert_fusion
  240.3 4.3 bitcast_add_fusion.1
  247.6 17.1 %all_to_all.47 = bf16[4,2,128,464]{2,3,1,0:T(8,128)(2,1)S(1)} all-to-all(bf16[4,2,128,464]{2,3,1,0:T(8,128)(2,1)S(1)} %bitcast_bitcast_fusion.1), channel_id=1, replica_groups=mesh['y'=4,'z'=8,'wid'=4,'ad'=2] {'wid'}, dimensions={0} | all-to-all | bytes 1900544 | tf_op jit(solution)/shard_map/all_to_all | solution.py:81
  265.1 17.2 %all_to_all.48 = bf16[8,128,464]{1,2,0:T(8,128)(2,1)S(1)} all-to-all(bf16[8,128,464]{1,2,0:T(8,128)(2,1)S(1)} %stack.15), channel_id=1, replica_groups=mesh['y'=4,'z'=8,'wid'=4,'ad'=2] {'ad','wid'}, dimensions={0} | all-to-all | bytes 1900544 | tf_op jit(solution)/shard_map/all_to_all | solution.py:85
  286.2 27.8 %reduce-scatter.11.cloned.1.call-done = bf16[256,1024]{1,0:T(8,128)(2,1)} async-done(((bf16[1024,1024]{1,0:T(8,128)(2,1)}), bf16[256,1024]{1,0:T(8,128)(2,1)}) %reduce-scatter.11.cloned.1.call-update) | async-done | bytes 524304 | tf_op jit(solution)/shard_map/reduce_scatter | solution.py:94
  314.0 39.8 %reduce-scatter.9.cloned.1.call-done = bf16[32,1024]{1,0:T(8,128)(2,1)} async-done(((bf16[256,1024]{1,0:T(8,128)(2,1)}), bf16[32,1024]{1,0:T(8,128)(2,1)}) %reduce-scatter.9.cloned.1.call-update) | async-done | bytes 65552 | tf_op jit(solution)/shard_map/reduce_scatter | solution.py:95
  353.8 38.7 %reduce-scatter.17.cloned.1.call-done = bf16[32,1024]{1,0:T(8,128)(2,1)} async-done(((bf16[256,1024]{1,0:T(8,128)(2,1)}), bf16[32,1024]{1,0:T(8,128)(2,1)}) %reduce-scatter.17.cloned.1.call-update) | async-done | bytes 65552 | tf_op jit(solution)/shard_map/reduce_scatter | solution.py:95
  392.5 38.7 %reduce-scatter.13.cloned.1.call-done = bf16[32,1024]{1,0:T(8,128)(2,1)} async-done(((bf16[256,1024]{1,0:T(8,128)(2,1)}), bf16[32,1024]{1,0:T(8,128)(2,1)}) %reduce-scatter.13.cloned.1.call-update) | async-done | bytes 65552 | tf_op jit(solution)/shard_map/reduce_scatter | solution.py:95
  (75 shorter events, 41.8 us)
Async XLA Ops:
  6.5 137.3 %copy-start = (bf16[1024,2,464]{0,2,1:T(8,128)(2,1)S(1)}, bf16[1024,2,464]{0,2,1:T(8,128)(2,1)}, u32[]{:S(2)}) copy-start(bf16[1024,2,464]{0,2,1:T(8,128)(2,1)} %param.8) | copy-start | bytes 5701636
  31.5 7.5 %copy-start.4 = (bf16[1,1,64,8192]{3,2,1,0:T(8,128)(2,1)S(1)}, bf16[1,1,64,8192]{3,2,1,0:T(8,128)(2,1)}, u32[]{:S(2)}) copy-start(bf16[1,1,64,8192]{3,2,1,0:T(8,128)(2,1)} %param.10) | copy-start | bytes 3145732
  32.7 21.0 %all-to-all-start = ((bf16[8,64,1024]{2,1,0:T(8,128)(2,1)}), bf16[8,64,1024]{2,1,0:T(8,128)(2,1)}, u32[]{:S(2)}, u32[]{:S(2)}) async-start(bf16[8,64,1024]{2,1,0:T(8,128)(2,1)} %bitcast.7), calls=%async_computation | async-start | bytes 2097152 | tf_op jit(solution)/shard_map/all_to_all | solution.py:46
  57.8 22.0 %all-to-all-start.1 = ((bf16[32,2,2048]{2,1,0:T(2,128)(2,1)}), bf16[32,2,2048]{2,1,0:T(2,128)(2,1)S(1)}, u32[]{:S(2)}, u32[]{:S(2)}) async-start(bf16[32,2,2048]{2,1,0:T(2,128)(2,1)} %reshape.135), calls=%async_computation.1 | async-start | bytes 524288 | tf_op jit(solution)/shard_map/all_to_all | solution.py:50
  79.8 58.0 %all-to-all-start.2 = ((bf16[32,64,464]{2,1,0:T(8,128)(2,1)}), bf16[32,64,464]{2,1,0:T(8,128)(2,1)}, u32[]{:S(2)}, u32[]{:S(2)}) async-start(bf16[32,64,464]{2,1,0:T(8,128)(2,1)} %bitcast.100), calls=%async_computation.2 | async-start | bytes 4194304 | tf_op jit(solution)/shard_map/all_to_all | solution.py:25
  140.1 1.3 copy-start.2
  141.4 2.4 copy-start.3
  146.0 1.8 copy-start.1
  148.0 2.7 collective-permute-start
  171.0 17.8 %all-to-all-start.4 = ((bf16[8,128,464]{1,2,0:T(8,128)(2,1)}), bf16[8,128,464]{1,2,0:T(8,128)(2,1)S(1)}, u32[]{:S(2)}, u32[]{:S(2)}) async-start(bf16[8,128,464]{1,2,0:T(8,128)(2,1)} %stack.13), calls=%async_computation.4 | async-start | bytes 1900544 | tf_op jit(solution)/shard_map/all_to_all | solution.py:85
  175.9 109.1 %reduce-scatter.7.cloned.1.call-start = ((), (), s32[]{:S(2)}) async-start(), calls=%async_computation.15 | async-start | bytes 2621440 | tf_op jit(solution)/shard_map/reduce_scatter | solution.py:94
  197.2 2.6 collective-permute-start.2
  218.4 17.8 %all-to-all-start.8 = ((bf16[8,128,464]{1,2,0:T(8,128)(2,1)}), bf16[8,128,464]{1,2,0:T(8,128)(2,1)S(1)}, u32[]{:S(2)}, u32[]{:S(2)}) async-start(bf16[8,128,464]{1,2,0:T(8,128)(2,1)} %stack.17), calls=%async_computation.12 | async-start | bytes 1900544 | tf_op jit(solution)/shard_map/all_to_all | solution.py:85
  223.3 62.3 %reduce-scatter.15.cloned.1.call-start = ((), (), s32[]{:S(2)}) async-start(), calls=%async_computation.19 | async-start | bytes 2621440 | tf_op jit(solution)/shard_map/reduce_scatter | solution.py:94
  240.0 73.9 %reduce-scatter.11.cloned.1.call-start = ((), (), s32[]{:S(2)}) async-start(), calls=%async_computation.17 | async-start | bytes 2621440 | tf_op jit(solution)/shard_map/reduce_scatter | solution.py:94
  244.8 2.6 collective-permute-start.1
  264.9 17.4 %copy-start.5 = (bf16[464,1024]{1,0:T(8,128)(2,1)S(1)}, bf16[464,1024]{1,0:T(8,128)(2,1)}, u32[]{:S(2)}) copy-start(bf16[464,1024]{1,0:T(8,128)(2,1)} %param.9) | copy-start | bytes 2850820
  284.9 68.9 %reduce-scatter.9.cloned.1.call-start = ((), (), s32[]{:S(2)}) async-start(), calls=%async_computation.16 | async-start | bytes 589824 | tf_op jit(solution)/shard_map/reduce_scatter | solution.py:95
  285.5 107.0 %reduce-scatter.17.cloned.1.call-start = ((), (), s32[]{:S(2)}) async-start(), calls=%async_computation.20 | async-start | bytes 589824 | tf_op jit(solution)/shard_map/reduce_scatter | solution.py:95
  286.1 145.1 %reduce-scatter.13.cloned.1.call-start = ((), (), s32[]{:S(2)}) async-start(), calls=%async_computation.18 | async-start | bytes 589824 | tf_op jit(solution)/shard_map/reduce_scatter | solution.py:95
Sparse Core Ops, SparseCore 0:
  192.8 29.2 reduce-scatter.6
  240.1 29.1 reduce-scatter.14
  285.1 28.8 reduce-scatter.10
  316.3 37.4 reduce-scatter.8
  356.2 36.2 reduce-scatter.16
  394.9 36.2 reduce-scatter.12
